TPU v7x, 256 devices: a whole 4x4x8 slice. The times are simulated.
256 devices in a mesh: lat: 32 (over x, z), lead: 8 (over y, core).
Axes of the slice: x: 4, y: 4, z: 8, core: 2. Of those that a mesh axis runs over, the one named last changes fastest.
Arguments:
- latent: bfloat16 [32, 256, 64, 256], P('lat', None, 'lead'), may hold values from -6 to 6
- conv_weight: bfloat16 [3, 3, 256, 256], replicated, may hold values from -0.125 to 0.125
- conv_bias: float32 [256], replicated, may hold values from -4 to 4
- norm_gain: float32 [256], replicated, may hold values from 0.1 to 1.9
- w_query: bfloat16 [256, 256], replicated, may hold values from -12 to 12
- w_key: bfloat16 [256, 256], replicated, may hold values from -0.25 to 0.25
- w_value: bfloat16 [256, 256], replicated, may hold values from -0.375 to 0.375
- w_out: bfloat16 [256, 256], replicated, may hold values from -0.375 to 0.375
Outputs:
- section_out: bfloat16 [32, 256, 64, 256], P('lat', None, 'lead')
All inputs are finite; a program needn't handle non-finite values.
Results may differ from a plain program's by a relative error of at most 0.014.
Values may be sent and summed in bfloat16 or wider, within the bound.
No kernel may reach another device: no remote copies, remote signals or barrier semaphores. Data moves between devices by JAX's collectives and lax.ppermute only.
A program may use at most 128 MiB of HBM per device.

v0:
```python
import math
import jax
import jax.numpy as jnp
from jax import lax
from jax.sharding import PartitionSpec as P

HD = 32


def padded_2(block, sides, width):
    for axis, dim in sides:
        count = lax.axis_size(axis)
        forward = [(i, i + 1) for i in range(count - 1)]
        backward = [(target, source) for source, target in forward]
        low = lax.ppermute(
            lax.slice_in_dim(block, block.shape[dim] - width, None, axis=dim), axis, forward
        )
        high = lax.ppermute(lax.slice_in_dim(block, 0, width, axis=dim), axis, backward)
        block = jnp.concatenate([low, block, high], axis=dim)
    return block


def attend(query, keys, values):
    chans = query.shape[-1]
    heads = chans // HD
    q_shape = query.shape
    query = query.reshape(-1, q_shape[-2], heads, HD)
    keys = keys.reshape(-1, keys.shape[-2], heads, HD)
    values = values.reshape(-1, values.shape[-2], heads, HD)
    scores = jnp.einsum(
        "pqhd,pkhd->phqk", query, keys, preferred_element_type=jnp.float32
    ) / math.sqrt(HD)
    top = jnp.max(scores, axis=-1, keepdims=True)
    expo = jnp.exp(scores - top)
    weights = (expo / jnp.sum(expo, axis=-1, keepdims=True)).astype(jnp.bfloat16)
    attended = jnp.einsum("phqk,pkhd->pqhd", weights, values, preferred_element_type=jnp.float32)
    return attended.astype(jnp.bfloat16).reshape(q_shape)


def project(normed, weight):
    shape = normed.shape
    flat = jnp.dot(normed.reshape(-1, shape[-1]), weight, preferred_element_type=jnp.float32)
    return flat.astype(jnp.bfloat16).reshape(shape)


def shards(latent, conv_weight, conv_bias, norm_gain, w_query, w_key, w_value, w_out):
    nrows, width, leads, chans = latent.shape
    extended = padded_2(latent, (("lat", 0),), 1)
    padded = jnp.pad(extended, ((0, 0), (1, 1), (0, 0), (0, 0)))
    acc = jnp.zeros((nrows * width * leads, chans), jnp.float32)
    for a in range(3):
        for b in range(3):
            piece = padded[a : a + nrows, b : b + width].reshape(-1, chans)
            acc = acc + jnp.dot(piece, conv_weight[a, b], preferred_element_type=jnp.float32)
    hidden = jax.nn.gelu(acc + conv_bias, approximate=True).astype(jnp.bfloat16)
    hidden_f = hidden.astype(jnp.float32)
    mean = jnp.mean(hidden_f, axis=-1, keepdims=True)
    var = jnp.mean((hidden_f - mean) ** 2, axis=-1, keepdims=True)
    normed = ((hidden_f - mean) * lax.rsqrt(var + 1e-05) * norm_gain).astype(jnp.bfloat16)
    normed = normed.reshape(nrows, width, leads, chans)
    block = lax.all_to_all(normed, "lead", split_axis=1, concat_axis=2, tiled=True)
    attended_px = attend(project(block, w_query), project(block, w_key), project(block, w_value))
    attended = lax.all_to_all(attended_px, "lead", split_axis=2, concat_axis=1, tiled=True)
    mixed = hidden_f + jnp.dot(
        attended.reshape(-1, chans), w_out, preferred_element_type=jnp.float32
    )
    return mixed.astype(jnp.bfloat16).reshape(nrows, width, leads, chans)


def solution(mesh):
    in_specs = (P("lat", None, "lead", None), P(), P(), P(), P(), P(), P(), P())
    out_specs = P("lat", None, "lead", None)
    return jax.shard_map(shards, mesh=mesh, in_specs=in_specs, out_specs=out_specs, check_vma=False)
```

profile of v0, /device:TPU:6, one launch (start us, length us, event | category | flops | bytes accessed | tf_op | source)
XLA Modules:
  0.0 127.0 jit_solution(6796232368115607537)
XLA Ops:
  0.0 8.1 %collective-permute-start.1 = (bf16[1,256,8,256]{3,2,1,0:T(8,128)(2,1)}, bf16[1,256,8,256]{3,2,1,0:T(8,128)(2,1)S(1)}, u32[]{:S(2)}, u32[]{:S(2)}) collective-permute-start(bf16[1,256,8,256]{3,2,1,0:T(8,128)(2,1)} %param.8), channel_id=1, source_target_pairs={{8,0},{16,8},{24,16},{32,24},{40,32},{48,40},{56,48},{64,56},{72,6... | collective-permute-start | bytes 3145736 | tf_op jit(solution)/shard_map/ppermute | solution.py:18
  8.2 1.9 %collective-permute-start = (bf16[1,256,8,256]{3,2,1,0:T(8,128)(2,1)}, bf16[1,256,8,256]{3,2,1,0:T(8,128)(2,1)S(1)}, u32[]{:S(2)}, u32[]{:S(2)}) collective-permute-start(bf16[1,256,8,256]{3,2,1,0:T(8,128)(2,1)} %param.8), channel_id=1, source_target_pairs={{0,8},{8,16},{16,24},{24,32},{32,40},{40,48},{48,56},{56,64},{64,7... | collective-permute-start | bytes 3145736 | tf_op jit(solution)/shard_map/ppermute | solution.py:15
  10.1 1.7 %fusion.46 = f32[2048,256]{1,0:T(8,128)S(1)} fusion(bf16[1,256,8,256]{3,2,1,0:T(8,128)(2,1)} %param.8, bf16[3,3,256,256]{3,2,1,0:T(8,128)(2,1)} %param.9), kind=kOutput, calls=%fused_computation.61 | convolution fusion | flops 268435456 | bytes 3276800 | tf_op jit(solution)/shard_map/dot_general | solution.py:54
  11.8 19.1 %collective-permute-done.1 = bf16[1,256,8,256]{3,2,1,0:T(8,128)(2,1)S(1)} collective-permute-done((bf16[1,256,8,256]{3,2,1,0:T(8,128)(2,1)}, bf16[1,256,8,256]{3,2,1,0:T(8,128)(2,1)S(1)}, u32[]{:S(2)}, u32[]{:S(2)}) %collective-permute-start.1) | collective-permute-done | bytes 1048608 | tf_op jit(solution)/shard_map/ppermute | solution.py:18
  30.9 6.1 %collective-permute-done = bf16[1,256,8,256]{3,2,1,0:T(8,128)(2,1)S(1)} collective-permute-done((bf16[1,256,8,256]{3,2,1,0:T(8,128)(2,1)}, bf16[1,256,8,256]{3,2,1,0:T(8,128)(2,1)S(1)}, u32[]{:S(2)}, u32[]{:S(2)}) %collective-permute-start) | collective-permute-done | bytes 1048608 | tf_op jit(solution)/shard_map/ppermute | solution.py:15
  40.9 1.7 %convert_reduce_fusion = (f32[2048]{0:T(1024)S(1)}, bf16[2048,256]{1,0:T(8,128)(2,1)S(1)}) fusion(f32[256]{0:T(256)S(1)} %copy-done.8, f32[2048,256]{1,0:T(8,128)S(1)} %fusion.39, f32[2048,256]{1,0:T(8,128)S(1)} %fusion.44, f32[2048,256]{1,0:T(8,128)S(1)} %fusion.40, bf16[3,3,256,256]{3,2,1,0:T(8,128)(2,1)S(1)} %copy-done.4, ...), kind=kOutput, calls=%fused_computation.17 | convolution fusion | flops 278919168 | bytes 19014656 | tf_op jit(solution)/shard_map/dot_general | solution.py:54
  42.6 0.6 fusion.19
  43.3 0.7 fusion.38
  44.0 20.4 %all_to_all.30 = bf16[1,256,8,256]{3,2,0,1:T(8,128)(2,1)S(1)} all-to-all(bf16[1,256,8,256]{3,2,0,1:T(8,128)(2,1)S(1)} %fusion.38), channel_id=1, replica_groups=mesh['lat'=32,'lead'=8] {'lead'}, dimensions={1} | all-to-all | bytes 2097152 | tf_op jit(solution)/shard_map/all_to_all | solution.py:61
  64.6 1.4 %convolution_convert_fusion = bf16[2048,256]{1,0:T(8,128)(2,1)} fusion(bf16[2048,256]{1,0:T(8,128)(2,1)S(1)} %bitcast.91, bf16[256,256]{1,0:T(8,128)(2,1)S(1)} %copy-done), kind=kOutput, calls=%fused_computation.25 | convolution fusion | flops 268959744 | bytes 2228224 | tf_op jit(solution)/shard_map/dot_general | solution.py:42
  66.0 1.5 %copy.36 = bf16[2048,256]{0,1:T(8,128)(2,1)S(1)} copy(bf16[2048,256]{1,0:T(8,128)(2,1)} %convolution_convert_fusion) | data formatting | bytes 2097152 | tf_op jit(solution)/shard_map/convert_element_type | solution.py:43
  67.5 3.2 %reshape_reshape.11 = bf16[32,64,8,32]{1,0,3,2:T(8,128)(2,1)} reshape(bf16[2048,256]{0,1:T(8,128)(2,1)S(1)} %copy.36) | data formatting | bytes 2097152 | tf_op jit(solution)/shard_map/reshape;reshape | solution.py:28
  71.1 1.4 %convolution_convert_fusion.2 = bf16[2048,256]{1,0:T(8,128)(2,1)} fusion(bf16[2048,256]{1,0:T(8,128)(2,1)S(1)} %bitcast.93, bf16[256,256]{1,0:T(8,128)(2,1)S(1)} %copy-done.6), kind=kOutput, calls=%fused_computation.27 | convolution fusion | flops 268959744 | bytes 2228224 | tf_op jit(solution)/shard_map/dot_general | solution.py:42
  72.5 2.3 %copy.34 = bf16[2048,256]{0,1:T(8,128)(2,1)} copy(bf16[2048,256]{1,0:T(8,128)(2,1)} %convolution_convert_fusion.2) | data formatting | bytes 2097152 | tf_op jit(solution)/shard_map/convert_element_type | solution.py:43
  74.8 0.6 copy.35
  75.4 3.2 %reshape_reshape.10 = bf16[32,64,8,32]{1,0,3,2:T(8,128)(2,1)} reshape(bf16[2048,256]{0,1:T(8,128)(2,1)S(1)} %copy.35) | data formatting | bytes 2097152 | tf_op jit(solution)/shard_map/reshape;reshape | solution.py:27
  78.6 4.6 %reshape_reshape.9 = bf16[32,64,8,32]{1,0,3,2:T(8,128)(2,1)} reshape(bf16[2048,256]{0,1:T(8,128)(2,1)} %copy.34) | data formatting | bytes 2097152 | tf_op jit(solution)/shard_map/reshape;reshape | solution.py:29
  83.2 4.4 %fusion.31 = f32[32,8,64,64]{2,3,1,0:T(8,128)S(1)} fusion(bf16[32,64,8,32]{1,0,3,2:T(8,128)(2,1)S(1)} %copy-done.1, bf16[32,64,8,32]{1,0,3,2:T(8,128)(2,1)} %reshape_reshape.10), kind=kOutput, calls=%fused_computation.42 | convolution fusion | flops 67108864 | bytes 6291456 | tf_op jit(solution)/shard_map/pqhd,pkhd->phqk/dot_general | solution.py:30
  87.5 12.2 %fusion.69 = (f32[32,8,64]{2,1,0:T(8,128)S(1)}, f32[32,8,64,64]{2,3,1,0:T(8,128)S(1)}) fusion(f32[32,8,64,64]{2,3,1,0:T(8,128)S(1)} %fusion.31), kind=kOutput, calls=%fused_computation.87 | output fusion | flops 4194367 | bytes 8454144 | tf_op jit(solution)/shard_map/sub | solution.py:34
  99.7 3.8 %fusion.34 = bf16[32,8,32,64]{3,2,1,0:T(8,128)(2,1)} fusion(f32[32,8,64,64]{2,3,1,0:T(8,128)S(1)} %get-tuple-element.8, f32[32,8,64]{2,1,0:T(8,128)S(1)} %get-tuple-element.7, bf16[32,64,8,32]{1,0,3,2:T(8,128)(2,1)S(1)} %copy-done.3), kind=kOutput, calls=%fused_computation.45 | convolution fusion | flops 69730304 | bytes 6356992 | tf_op jit(solution)/shard_map/phqk,pkhd->pqhd/dot_general | solution.py:36
  103.5 2.7 %copy.41 = bf16[1,32,64,256]{3,1,0,2:T(8,128)(2,1)S(1)} copy(bf16[1,32,64,256]{2,3,1,0:T(8,128)(2,1)} %bitcast.97) | data formatting | bytes 2097152 | tf_op jit(solution)/shard_map/reshape | solution.py:37
  106.2 18.5 %all_to_all.31 = bf16[1,32,64,256]{3,1,0,2:T(8,128)(2,1)S(1)} all-to-all(bf16[1,32,64,256]{3,1,0,2:T(8,128)(2,1)S(1)} %copy.41), channel_id=1, replica_groups=mesh['lat'=32,'lead'=8] {'lead'}, dimensions={2} | all-to-all | bytes 2097152 | tf_op jit(solution)/shard_map/all_to_all | solution.py:63
  124.7 0.6 copy.54
  125.6 1.4 %fusion.37 = bf16[1,256,8,256]{3,2,1,0:T(8,128)(2,1)} fusion(bf16[2048,256]{1,0:T(8,128)(2,1)S(1)} %bitcast.94, bf16[256,256]{1,0:T(8,128)(2,1)S(1)} %copy-done.7, bf16[2048,256]{1,0:T(8,128)(2,1)S(1)} %get-tuple-element.6), kind=kOutput, calls=%fused_computation.46 | convolution fusion | flops 270008320 | bytes 3276800 | tf_op jit(solution)/shard_map/dot_general | solution.py:64
  (33 shorter events, 4.7 us)
Async XLA Ops:
  0.0 64.5 %copy-start = (bf16[256,256]{1,0:T(8,128)(2,1)S(1)}, bf16[256,256]{1,0:T(8,128)(2,1)}, u32[]{:S(2)}) copy-start(bf16[256,256]{1,0:T(8,128)(2,1)} %param.13) | copy-start | bytes 393220
  0.0 37.0 %copy-start.2 = (bf16[1,256,8,256]{3,2,1,0:T(8,128)(2,1)S(1)}, bf16[1,256,8,256]{3,2,1,0:T(8,128)(2,1)}, u32[]{:S(2)}) copy-start(bf16[1,256,8,256]{3,2,1,0:T(8,128)(2,1)} %param.8) | copy-start | bytes 3145732
  0.0 30.9 %collective-permute-start.1 = (bf16[1,256,8,256]{3,2,1,0:T(8,128)(2,1)}, bf16[1,256,8,256]{3,2,1,0:T(8,128)(2,1)S(1)}, u32[]{:S(2)}, u32[]{:S(2)}) collective-permute-start(bf16[1,256,8,256]{3,2,1,0:T(8,128)(2,1)} %param.8), channel_id=1, source_target_pairs={{8,0},{16,8},{24,16},{32,24},{40,32},{48,40},{56,48},{64,56},{72,6... | collective-permute-start | bytes 3145736 | tf_op jit(solution)/shard_map/ppermute | solution.py:18
  8.2 28.8 %collective-permute-start = (bf16[1,256,8,256]{3,2,1,0:T(8,128)(2,1)}, bf16[1,256,8,256]{3,2,1,0:T(8,128)(2,1)S(1)}, u32[]{:S(2)}, u32[]{:S(2)}) collective-permute-start(bf16[1,256,8,256]{3,2,1,0:T(8,128)(2,1)} %param.8), channel_id=1, source_target_pairs={{0,8},{8,16},{16,24},{24,32},{32,40},{40,48},{48,56},{56,64},{64,7... | collective-permute-start | bytes 3145736 | tf_op jit(solution)/shard_map/ppermute | solution.py:15
  11.8 25.8 %copy-start.4 = (bf16[3,3,256,256]{3,2,1,0:T(8,128)(2,1)S(1)}, bf16[3,3,256,256]{3,2,1,0:T(8,128)(2,1)}, u32[]{:S(2)}) copy-start(bf16[3,3,256,256]{3,2,1,0:T(8,128)(2,1)} %param.9) | copy-start | bytes 3538948
  40.2 0.7 copy-start.8
  40.9 2.4 %copy-start.9 = (f32[256]{0:T(256)S(1)}, f32[256]{0:T(256)}, u32[]{:S(2)}) copy-start(f32[256]{0:T(256)} %param.11) | copy-start | bytes 3076
  67.4 3.2 %copy-start.5 = (bf16[256,256]{1,0:T(8,128)(2,1)S(1)}, bf16[256,256]{1,0:T(8,128)(2,1)}, u32[]{:S(2)}) copy-start(bf16[256,256]{1,0:T(8,128)(2,1)} %param.12) | copy-start | bytes 393220
  67.5 3.7 %copy-start.6 = (bf16[256,256]{1,0:T(8,128)(2,1)S(1)}, bf16[256,256]{1,0:T(8,128)(2,1)}, u32[]{:S(2)}) copy-start(bf16[256,256]{1,0:T(8,128)(2,1)} %param.14) | copy-start | bytes 393220
  78.6 4.6 %copy-start.1 = (bf16[32,64,8,32]{1,0,3,2:T(8,128)(2,1)S(1)}, bf16[32,64,8,32]{1,0,3,2:T(8,128)(2,1)}, u32[]{:S(2)}) copy-start(bf16[32,64,8,32]{1,0,3,2:T(8,128)(2,1)} %reshape_reshape.11) | copy-start | bytes 3145732
  87.5 12.2 %copy-start.3 = (bf16[32,64,8,32]{1,0,3,2:T(8,128)(2,1)S(1)}, bf16[32,64,8,32]{1,0,3,2:T(8,128)(2,1)}, u32[]{:S(2)}) copy-start(bf16[32,64,8,32]{1,0,3,2:T(8,128)(2,1)} %reshape_reshape.9) | copy-start | bytes 3145732
  124.7 0.9 copy-start.7
where the time goes:
time: 127 us
  blocking collectives  38.9 us (31%)
  waiting for transfers between devices  25.2 us (20%)
  local copies, waits for them, and re-layouts  19.3 us (15%)
  matrix products  19.2 us (15%)
  other arithmetic  14.1 us (11%)
  starting transfers between devices  10.1 us (8%)
    all_to_all x1, blocking collectives, shards(): lax.all_to_all(normed, 'lead', split_axis=1, concat_axis=2, tiled=True)  20.4 us
    ppermute x1, waiting for transfers between devices, padded_2(): lax.ppermute(lax.slice_in_dim(block, 0, width, axis=dim), axis, backward)  19.1 us
    all_to_all x1, blocking collectives, shards(): lax.all_to_all(attended_px, 'lead', split_axis=2, concat_axis=1, tiled=True)  18.5 us
    sub x1, other arithmetic, attend(): expo = jnp.exp(scores - top)  12.2 us
    ppermute x1, starting transfers between devices, padded_2(): lax.ppermute(lax.slice_in_dim(block, 0, width, axis=dim), axis, backward)  8.15 us
    dot_general x9, matrix products, shards(): jnp.dot(piece, conv_weight[a, b], preferred_element_type=jnp.float32)  6.44 us
    ppermute x1, waiting for transfers between devices, padded_2(): lax.ppermute(lax.slice_in_dim(block, block.shape[dim] - width, None, axis...  6.12 us
    another operation x1, local copies, waits for them, and re-layouts, attend(): values = values.reshape(-1, values.shape[-2], heads, HD)  4.55 us
  transfers between devices with their start and end apart: 2, of which 2 were waited for; matrix products, arithmetic and copies ran while one was open for 1% of the time, Pallas kernels for 0%

commit v1 on v0

--- a/solution.py
+++ b/solution.py
@@ -5,6 +5,18 @@
 from jax.sharding import PartitionSpec as P
 
 HD = 32
+
+
+def split_up(shard, dim, length):
+    lengths = shard.shape
+    blocks = shard.reshape(*lengths[:dim], length, lengths[dim] // length, *lengths[dim + 1 :])
+    return jnp.moveaxis(blocks, dim, 0)
+
+
+def laid_out(blocks, dim):
+    shape = list(blocks.shape[1:])
+    shape[dim] *= blocks.shape[0]
+    return jnp.moveaxis(blocks, 0, dim).reshape(shape)
 
 
 def padded_2(block, sides, width):
@@ -58,7 +70,17 @@
     var = jnp.mean((hidden_f - mean) ** 2, axis=-1, keepdims=True)
     normed = ((hidden_f - mean) * lax.rsqrt(var + 1e-05) * norm_gain).astype(jnp.bfloat16)
     normed = normed.reshape(nrows, width, leads, chans)
-    block = lax.all_to_all(normed, "lead", split_axis=1, concat_axis=2, tiled=True)
+    count_2, place = (lax.axis_size("lead"), lax.axis_index("lead"))
+    tiles = split_up(normed, 1, count_2)
+    out = tiles
+    for step in range(1, count_2):
+        target_2, source_2 = ((place + step) % count_2, (place - step) % count_2)
+        sent = lax.dynamic_index_in_dim(tiles, target_2, 0)
+        theirs = lax.ppermute(
+            sent, "lead", [(i_2, (i_2 + step) % count_2) for i_2 in range(count_2)]
+        )
+        out = lax.dynamic_update_slice_in_dim(out, theirs, source_2, axis=0)
+    block = laid_out(out, 2)
     attended_px = attend(project(block, w_query), project(block, w_key), project(block, w_value))
     attended = lax.all_to_all(attended_px, "lead", split_axis=2, concat_axis=1, tiled=True)
     mixed = hidden_f + jnp.dot(

time: 127 us -> 123 us (0.969)
  blocking collectives: 38.9 us -> 20.3 us
  starting transfers between devices: 10.1 us -> 19 us
  other arithmetic: 14.1 us -> 6.43 us
  matrix products: 19.2 us -> 24.9 us
  waiting for transfers between devices: 25.2 us -> 30.5 us
  local copies, waits for them, and re-layouts: 19.3 us -> 21.4 us
    all_to_all x1 -> x0, blocking collectives: 20.4 us -> none  [shards(): lax.all_to_all(normed, 'lead', split_axis=1, concat_axis=2, tiled=True)]
    ppermute x0 -> x7, starting transfers between devices: none -> 8.97 us  [shards(): lax.ppermute(sent, 'lead', [(i_2, (i_2 + step) % count_2) for i_2 in rang...]
    sub x1, other arithmetic: 12.2 us -> 4.49 us  [attend(): expo = jnp.exp(scores - top)]
    ppermute x0 -> x7, waiting for transfers between devices: none -> 5.32 us  [shards(): lax.ppermute(sent, 'lead', [(i_2, (i_2 + step) % count_2) for i_2 in rang...]
    dot_general x1, matrix products: 3.8 us -> 7.81 us  [attend(): jnp.einsum('phqk,pkhd->pqhd', weights, values, preferred_element_type=jnp...]
    dynamic_update_slice x0 -> x7, local copies, waits for them, and re-layouts: none -> 1.89 us  [shards(): out = lax.dynamic_update_slice_in_dim(out, theirs, source_2, axis=0)]
    all_to_all x1, blocking collectives: 18.5 us -> 20.3 us  [shards(): lax.all_to_all(attended_px, 'lead', split_axis=2, concat_axis=1, tiled=True)]
    another operation x1, local copies, waits for them, and re-layouts: 4.55 us -> 3.13 us  [attend(): values = values.reshape(-1, values.shape[-2], heads, HD)]
  transfers between devices with their start and end apart: 2 -> 9, of which waited for: 2 -> 6; matrix products, arithmetic and copies ran while one was open for 1% -> 3% of each run, Pallas kernels for 0% -> 0%
where the time goes in v1:
time: 123 us
  waiting for transfers between devices  30.5 us (25%)
  matrix products  24.9 us (20%)
  local copies, waits for them, and re-layouts  21.4 us (17%)
  blocking collectives  20.3 us (17%)
  starting transfers between devices  19 us (15%)
  other arithmetic  6.43 us (5%)
    all_to_all x1, blocking collectives, shards(): lax.all_to_all(attended_px, 'lead', split_axis=2, concat_axis=1, tiled=True)  20.3 us
    ppermute x1, waiting for transfers between devices, padded_2(): lax.ppermute(lax.slice_in_dim(block, 0, width, axis=dim), axis, backward)  19 us
    ppermute x7, starting transfers between devices, shards(): lax.ppermute(sent, 'lead', [(i_2, (i_2 + step) % count_2) for i_2 in rang...  8.97 us
    ppermute x1, starting transfers between devices, padded_2(): lax.ppermute(lax.slice_in_dim(block, 0, width, axis=dim), axis, backward)  8.15 us
    dot_general x1, matrix products, attend(): jnp.einsum('phqk,pkhd->pqhd', weights, values, preferred_element_type=jnp...  7.81 us
    dot_general x9, matrix products, shards(): jnp.dot(piece, conv_weight[a, b], preferred_element_type=jnp.float32)  6.44 us
    ppermute x1, waiting for transfers between devices, padded_2(): lax.ppermute(lax.slice_in_dim(block, block.shape[dim] - width, None, axis...  6.12 us
    ppermute x7, waiting for transfers between devices, shards(): lax.ppermute(sent, 'lead', [(i_2, (i_2 + step) % count_2) for i_2 in rang...  5.32 us
  transfers between devices with their start and end apart: 9, of which 6 were waited for; matrix products, arithmetic and copies ran while one was open for 3% of the time, Pallas kernels for 0%

profile of v1, /device:TPU:6, one launch (start us, length us, event | category | flops | bytes accessed | tf_op | source)
XLA Modules:
  0.0 122.9 jit_solution(2303123911685074144)
XLA Ops:
  0.0 8.1 %collective-permute-start.1 = (bf16[1,256,8,256]{3,2,1,0:T(8,128)(2,1)}, bf16[1,256,8,256]{3,2,1,0:T(8,128)(2,1)S(1)}, u32[]{:S(2)}, u32[]{:S(2)}) collective-permute-start(bf16[1,256,8,256]{3,2,1,0:T(8,128)(2,1)} %param.8), channel_id=1, source_target_pairs={{8,0},{16,8},{24,16},{32,24},{40,32},{48,40},{56,48},{64,56},{72,6... | collective-permute-start | bytes 3145736 | tf_op jit(solution)/shard_map/ppermute | solution.py:30
  8.2 1.9 %collective-permute-start = (bf16[1,256,8,256]{3,2,1,0:T(8,128)(2,1)}, bf16[1,256,8,256]{3,2,1,0:T(8,128)(2,1)S(1)}, u32[]{:S(2)}, u32[]{:S(2)}) collective-permute-start(bf16[1,256,8,256]{3,2,1,0:T(8,128)(2,1)} %param.8), channel_id=1, source_target_pairs={{0,8},{8,16},{16,24},{24,32},{32,40},{40,48},{48,56},{56,64},{64,7... | collective-permute-start | bytes 3145736 | tf_op jit(solution)/shard_map/ppermute | solution.py:27
  10.2 1.7 %fusion.45 = f32[2048,256]{1,0:T(8,128)S(1)} fusion(bf16[1,256,8,256]{3,2,1,0:T(8,128)(2,1)} %param.8, bf16[3,3,256,256]{3,2,1,0:T(8,128)(2,1)} %param.9), kind=kOutput, calls=%fused_computation.60 | convolution fusion | flops 268435456 | bytes 3276800 | tf_op jit(solution)/shard_map/dot_general | solution.py:66
  11.9 19.0 %collective-permute-done.1 = bf16[1,256,8,256]{3,2,1,0:T(8,128)(2,1)S(1)} collective-permute-done((bf16[1,256,8,256]{3,2,1,0:T(8,128)(2,1)}, bf16[1,256,8,256]{3,2,1,0:T(8,128)(2,1)S(1)}, u32[]{:S(2)}, u32[]{:S(2)}) %collective-permute-start.1) | collective-permute-done | bytes 1048608 | tf_op jit(solution)/shard_map/ppermute | solution.py:30
  30.9 6.1 %collective-permute-done = bf16[1,256,8,256]{3,2,1,0:T(8,128)(2,1)S(1)} collective-permute-done((bf16[1,256,8,256]{3,2,1,0:T(8,128)(2,1)}, bf16[1,256,8,256]{3,2,1,0:T(8,128)(2,1)S(1)}, u32[]{:S(2)}, u32[]{:S(2)}) %collective-permute-start) | collective-permute-done | bytes 1048608 | tf_op jit(solution)/shard_map/ppermute | solution.py:27
  40.9 1.7 %convert_reduce_fusion = (f32[2048]{0:T(1024)S(1)}, bf16[2048,256]{1,0:T(8,128)(2,1)S(1)}) fusion(f32[256]{0:T(256)S(1)} %copy-done.9, f32[2048,256]{1,0:T(8,128)S(1)} %fusion.38, f32[2048,256]{1,0:T(8,128)S(1)} %fusion.43, f32[2048,256]{1,0:T(8,128)S(1)} %fusion.39, bf16[3,3,256,256]{3,2,1,0:T(8,128)(2,1)S(1)} %copy-done.2, ...), kind=kOutput, calls=%fused_computation.17 | convolution fusion | flops 278919168 | bytes 19014656 | tf_op jit(solution)/shard_map/dot_general | solution.py:66
  44.9 1.6 %collective-permute-start.3 = (bf16[1,1,32,8,256]{4,3,0,2,1:T(8,128)(2,1)}, bf16[1,1,32,8,256]{4,3,0,2,1:T(8,128)(2,1)}, u32[]{:S(2)}, u32[]{:S(2)}) collective-permute-start(bf16[1,1,32,8,256]{4,3,0,2,1:T(8,128)(2,1)} %get-tuple-element.10), channel_id=1, source_target_pairs={{0,2},{1,3},{2,4},{3,5},{4,6},{5,7},{6,0},{7,1},{8,10},{9,11},{10,... | collective-permute-start | bytes 393224 | tf_op jit(solution)/shard_map/ppermute | solution.py:79
  47.4 2.3 %collective-permute-start.4 = (bf16[1,1,32,8,256]{4,3,0,2,1:T(8,128)(2,1)S(1)}, bf16[1,1,32,8,256]{4,3,0,2,1:T(8,128)(2,1)S(1)}, u32[]{:S(2)}, u32[]{:S(2)}) collective-permute-start(bf16[1,1,32,8,256]{4,3,0,2,1:T(8,128)(2,1)S(1)} %copy-done.8), channel_id=1, source_target_pairs={{0,3},{1,4},{2,5},{3,6},{4,7},{5,0},{6,1},{7,2},{8,11},{9,12},{10,... | collective-permute-start | bytes 393224 | tf_op jit(solution)/shard_map/ppermute | solution.py:79
  49.7 1.8 %collective-permute-start.5 = (bf16[1,1,32,8,256]{4,3,0,2,1:T(8,128)(2,1)S(1)}, bf16[1,1,32,8,256]{4,3,0,2,1:T(8,128)(2,1)S(1)}, u32[]{:S(2)}, u32[]{:S(2)}) collective-permute-start(bf16[1,1,32,8,256]{4,3,0,2,1:T(8,128)(2,1)S(1)} %copy-done.7), channel_id=1, source_target_pairs={{0,4},{1,5},{2,6},{3,7},{4,0},{5,1},{6,2},{7,3},{8,12},{9,13},{10,... | collective-permute-start | bytes 393224 | tf_op jit(solution)/shard_map/ppermute | solution.py:79
  51.5 1.8 %collective-permute-start.6 = (bf16[1,1,32,8,256]{4,3,0,2,1:T(8,128)(2,1)S(1)}, bf16[1,1,32,8,256]{4,3,0,2,1:T(8,128)(2,1)S(1)}, u32[]{:S(2)}, u32[]{:S(2)}) collective-permute-start(bf16[1,1,32,8,256]{4,3,0,2,1:T(8,128)(2,1)S(1)} %copy-done.6), channel_id=1, source_target_pairs={{0,5},{1,6},{2,7},{3,0},{4,1},{5,2},{6,3},{7,4},{8,13},{9,14},{10,... | collective-permute-start | bytes 393224 | tf_op jit(solution)/shard_map/ppermute | solution.py:79
  56.6 1.8 %collective-permute-done.4 = bf16[1,1,32,8,256]{4,3,0,2,1:T(8,128)(2,1)S(1)} collective-permute-done((bf16[1,1,32,8,256]{4,3,0,2,1:T(8,128)(2,1)S(1)}, bf16[1,1,32,8,256]{4,3,0,2,1:T(8,128)(2,1)S(1)}, u32[]{:S(2)}, u32[]{:S(2)}) %collective-permute-start.4) | collective-permute-done | bytes 131104 | tf_op jit(solution)/shard_map/ppermute | solution.py:79
  59.6 2.1 %collective-permute-done.7 = bf16[1,1,32,8,256]{4,3,0,2,1:T(8,128)(2,1)S(1)} collective-permute-done((bf16[1,1,32,8,256]{4,3,0,2,1:T(8,128)(2,1)S(1)}, bf16[1,1,32,8,256]{4,3,0,2,1:T(8,128)(2,1)S(1)}, u32[]{:S(2)}, u32[]{:S(2)}) %collective-permute-start.7) | collective-permute-done | bytes 131104 | tf_op jit(solution)/shard_map/ppermute | solution.py:79
  62.0 1.4 %convolution_convert_fusion = bf16[2048,256]{1,0:T(8,128)(2,1)} fusion(bf16[2048,256]{1,0:T(8,128)(2,1)S(1)} %bitcast.87, bf16[256,256]{1,0:T(8,128)(2,1)S(1)} %copy-done), kind=kOutput, calls=%fused_computation.25 | convolution fusion | flops 268959744 | bytes 2228224 | tf_op jit(solution)/shard_map/dot_general | solution.py:54
  63.4 1.5 %copy.40 = bf16[2048,256]{0,1:T(8,128)(2,1)S(1)} copy(bf16[2048,256]{1,0:T(8,128)(2,1)} %convolution_convert_fusion) | data formatting | bytes 2097152 | tf_op jit(solution)/shard_map/convert_element_type | solution.py:55
  64.9 3.2 %reshape_reshape.17 = bf16[32,64,8,32]{1,0,3,2:T(8,128)(2,1)} reshape(bf16[2048,256]{0,1:T(8,128)(2,1)S(1)} %copy.40) | data formatting | bytes 2097152 | tf_op jit(solution)/shard_map/reshape;reshape | solution.py:40
  69.5 1.5 %copy.39 = bf16[2048,256]{0,1:T(8,128)(2,1)S(1)} copy(bf16[2048,256]{1,0:T(8,128)(2,1)} %convolution_convert_fusion.1) | data formatting | bytes 2097152 | tf_op jit(solution)/shard_map/convert_element_type | solution.py:55
  71.0 3.2 %reshape_reshape.16 = bf16[32,64,8,32]{1,0,3,2:T(8,128)(2,1)} reshape(bf16[2048,256]{0,1:T(8,128)(2,1)S(1)} %copy.39) | data formatting | bytes 2097152 | tf_op jit(solution)/shard_map/reshape;reshape | solution.py:39
  74.2 5.0 %fusion.31 = f32[32,8,64,64]{2,3,1,0:T(8,128)S(1)} fusion(bf16[32,64,8,32]{1,0,3,2:T(8,128)(2,1)} %reshape_reshape.17, bf16[32,64,8,32]{1,0,3,2:T(8,128)(2,1)} %reshape_reshape.16), kind=kOutput, calls=%fused_computation.42 | convolution fusion | flops 67108864 | bytes 6291456 | tf_op jit(solution)/shard_map/pqhd,pkhd->phqk/dot_general | solution.py:42
  79.3 4.5 %fusion.68 = (f32[32,8,64]{2,1,0:T(8,128)S(1)}, f32[32,8,64,64]{2,3,1,0:T(8,128)}) fusion(f32[32,8,64,64]{2,3,1,0:T(8,128)S(1)} %fusion.31), kind=kOutput, calls=%fused_computation.100 | output fusion | flops 4194367 | bytes 8454144 | tf_op jit(solution)/shard_map/sub | solution.py:46
  85.1 1.5 %copy.38 = bf16[2048,256]{0,1:T(8,128)(2,1)S(1)} copy(bf16[2048,256]{1,0:T(8,128)(2,1)} %convolution_convert_fusion.2) | data formatting | bytes 2097152 | tf_op jit(solution)/shard_map/convert_element_type | solution.py:55
  86.6 3.1 %reshape_reshape.15 = bf16[32,64,8,32]{1,0,3,2:T(8,128)(2,1)} reshape(bf16[2048,256]{0,1:T(8,128)(2,1)S(1)} %copy.38) | data formatting | bytes 2097152 | tf_op jit(solution)/shard_map/reshape;reshape | solution.py:41
  89.8 7.8 %fusion.34 = bf16[32,8,32,64]{3,2,1,0:T(8,128)(2,1)} fusion(f32[32,8,64,64]{2,3,1,0:T(8,128)} %get-tuple-element.15, f32[32,8,64]{2,1,0:T(8,128)S(1)} %get-tuple-element.14, bf16[32,64,8,32]{1,0,3,2:T(8,128)(2,1)} %reshape_reshape.15), kind=kOutput, calls=%fused_computation.45 | convolution fusion | flops 69730304 | bytes 6356992 | tf_op jit(solution)/shard_map/phqk,pkhd->pqhd/dot_general | solution.py:48
  97.6 2.7 %copy.45 = bf16[1,32,64,256]{3,1,0,2:T(8,128)(2,1)S(1)} copy(bf16[1,32,64,256]{2,3,1,0:T(8,128)(2,1)} %bitcast.94) | data formatting | bytes 2097152 | tf_op jit(solution)/shard_map/reshape | solution.py:49
  100.3 20.3 %all_to_all.15 = bf16[1,32,64,256]{3,1,0,2:T(8,128)(2,1)S(1)} all-to-all(bf16[1,32,64,256]{3,1,0,2:T(8,128)(2,1)S(1)} %copy.45), channel_id=1, replica_groups=mesh['lat'=32,'lead'=8] {'lead'}, dimensions={2} | all-to-all | bytes 2097152 | tf_op jit(solution)/shard_map/all_to_all | solution.py:85
  (56 shorter events, 16.9 us)
Async XLA Ops:
  0.0 62.0 %copy-start = (bf16[256,256]{1,0:T(8,128)(2,1)S(1)}, bf16[256,256]{1,0:T(8,128)(2,1)}, u32[]{:S(2)}) copy-start(bf16[256,256]{1,0:T(8,128)(2,1)} %param.13) | copy-start | bytes 393220
  0.0 37.0 %copy-start.1 = (bf16[1,256,8,256]{3,2,1,0:T(8,128)(2,1)S(1)}, bf16[1,256,8,256]{3,2,1,0:T(8,128)(2,1)}, u32[]{:S(2)}) copy-start(bf16[1,256,8,256]{3,2,1,0:T(8,128)(2,1)} %param.8) | copy-start | bytes 3145732
  0.0 30.9 %collective-permute-start.1 = (bf16[1,256,8,256]{3,2,1,0:T(8,128)(2,1)}, bf16[1,256,8,256]{3,2,1,0:T(8,128)(2,1)S(1)}, u32[]{:S(2)}, u32[]{:S(2)}) collective-permute-start(bf16[1,256,8,256]{3,2,1,0:T(8,128)(2,1)} %param.8), channel_id=1, source_target_pairs={{8,0},{16,8},{24,16},{32,24},{40,32},{48,40},{56,48},{64,56},{72,6... | collective-permute-start | bytes 3145736 | tf_op jit(solution)/shard_map/ppermute | solution.py:30
  8.2 28.8 %collective-permute-start = (bf16[1,256,8,256]{3,2,1,0:T(8,128)(2,1)}, bf16[1,256,8,256]{3,2,1,0:T(8,128)(2,1)S(1)}, u32[]{:S(2)}, u32[]{:S(2)}) collective-permute-start(bf16[1,256,8,256]{3,2,1,0:T(8,128)(2,1)} %param.8), channel_id=1, source_target_pairs={{0,8},{8,16},{16,24},{24,32},{32,40},{40,48},{48,56},{56,64},{64,7... | collective-permute-start | bytes 3145736 | tf_op jit(solution)/shard_map/ppermute | solution.py:27
  11.8 25.7 %copy-start.2 = (bf16[3,3,256,256]{3,2,1,0:T(8,128)(2,1)S(1)}, bf16[3,3,256,256]{3,2,1,0:T(8,128)(2,1)}, u32[]{:S(2)}) copy-start(bf16[3,3,256,256]{3,2,1,0:T(8,128)(2,1)} %param.9) | copy-start | bytes 3538948
  40.2 0.7 copy-start.9
  40.9 2.4 %copy-start.10 = (f32[256]{0:T(256)S(1)}, f32[256]{0:T(256)}, u32[]{:S(2)}) copy-start(f32[256]{0:T(256)} %param.11) | copy-start | bytes 3076
  44.9 8.4 %collective-permute-start.2 = (bf16[1,1,32,8,256]{4,3,0,2,1:T(8,128)(2,1)}, bf16[1,1,32,8,256]{4,3,0,2,1:T(8,128)(2,1)}, u32[]{:S(2)}, u32[]{:S(2)}) collective-permute-start(bf16[1,1,32,8,256]{4,3,0,2,1:T(8,128)(2,1)} %get-tuple-element.11), channel_id=1, source_target_pairs={{0,1},{1,2},{2,3},{3,4},{4,5},{5,6},{6,7},{7,0},{8,9},{9,10},{10,1... | collective-permute-start | bytes 393224 | tf_op jit(solution)/shard_map/ppermute | solution.py:79
  44.9 10.7 %collective-permute-start.3 = (bf16[1,1,32,8,256]{4,3,0,2,1:T(8,128)(2,1)}, bf16[1,1,32,8,256]{4,3,0,2,1:T(8,128)(2,1)}, u32[]{:S(2)}, u32[]{:S(2)}) collective-permute-start(bf16[1,1,32,8,256]{4,3,0,2,1:T(8,128)(2,1)} %get-tuple-element.10), channel_id=1, source_target_pairs={{0,2},{1,3},{2,4},{3,5},{4,6},{5,7},{6,0},{7,1},{8,10},{9,11},{10,... | collective-permute-start | bytes 393224 | tf_op jit(solution)/shard_map/ppermute | solution.py:79
  46.5 0.9 copy-start.8
  46.5 3.2 %copy-start.7 = (bf16[1,1,32,8,256]{4,3,0,2,1:T(8,128)(2,1)S(1)}, bf16[1,1,32,8,256]{4,3,0,2,1:T(8,128)(2,1)}, u32[]{:S(2)}) copy-start(bf16[1,1,32,8,256]{4,3,0,2,1:T(8,128)(2,1)} %get-tuple-element.8) | copy-start | bytes 393220
  46.5 5.0 %copy-start.6 = (bf16[1,1,32,8,256]{4,3,0,2,1:T(8,128)(2,1)S(1)}, bf16[1,1,32,8,256]{4,3,0,2,1:T(8,128)(2,1)}, u32[]{:S(2)}) copy-start(bf16[1,1,32,8,256]{4,3,0,2,1:T(8,128)(2,1)} %get-tuple-element.7) | copy-start | bytes 393220
  47.4 11.0 %collective-permute-start.4 = (bf16[1,1,32,8,256]{4,3,0,2,1:T(8,128)(2,1)S(1)}, bf16[1,1,32,8,256]{4,3,0,2,1:T(8,128)(2,1)S(1)}, u32[]{:S(2)}, u32[]{:S(2)}) collective-permute-start(bf16[1,1,32,8,256]{4,3,0,2,1:T(8,128)(2,1)S(1)} %copy-done.8), channel_id=1, source_target_pairs={{0,3},{1,4},{2,5},{3,6},{4,7},{5,0},{6,1},{7,2},{8,11},{9,12},{10,... | collective-permute-start | bytes 393224 | tf_op jit(solution)/shard_map/ppermute | solution.py:79
  49.7 9.8 %collective-permute-start.5 = (bf16[1,1,32,8,256]{4,3,0,2,1:T(8,128)(2,1)S(1)}, bf16[1,1,32,8,256]{4,3,0,2,1:T(8,128)(2,1)S(1)}, u32[]{:S(2)}, u32[]{:S(2)}) collective-permute-start(bf16[1,1,32,8,256]{4,3,0,2,1:T(8,128)(2,1)S(1)} %copy-done.7), channel_id=1, source_target_pairs={{0,4},{1,5},{2,6},{3,7},{4,0},{5,1},{6,2},{7,3},{8,12},{9,13},{10,... | collective-permute-start | bytes 393224 | tf_op jit(solution)/shard_map/ppermute | solution.py:79
  51.5 8.0 %collective-permute-start.6 = (bf16[1,1,32,8,256]{4,3,0,2,1:T(8,128)(2,1)S(1)}, bf16[1,1,32,8,256]{4,3,0,2,1:T(8,128)(2,1)S(1)}, u32[]{:S(2)}, u32[]{:S(2)}) collective-permute-start(bf16[1,1,32,8,256]{4,3,0,2,1:T(8,128)(2,1)S(1)} %copy-done.6), channel_id=1, source_target_pairs={{0,5},{1,6},{2,7},{3,0},{4,1},{5,2},{6,3},{7,4},{8,13},{9,14},{10,... | collective-permute-start | bytes 393224 | tf_op jit(solution)/shard_map/ppermute | solution.py:79
  53.3 8.3 %collective-permute-start.7 = (bf16[1,1,32,8,256]{4,3,0,2,1:T(8,128)(2,1)S(1)}, bf16[1,1,32,8,256]{4,3,0,2,1:T(8,128)(2,1)S(1)}, u32[]{:S(2)}, u32[]{:S(2)}) collective-permute-start(bf16[1,1,32,8,256]{4,3,0,2,1:T(8,128)(2,1)S(1)} %get-tuple-element.6), channel_id=1, source_target_pairs={{0,6},{1,7},{2,0},{3,1},{4,2},{5,3},{6,4},{7,5},{8,14},{9,15},{10,... | collective-permute-start | bytes 393224 | tf_op jit(solution)/shard_map/ppermute | solution.py:79
  55.6 6.4 %collective-permute-start.8 = (bf16[1,1,32,8,256]{4,3,0,2,1:T(8,128)(2,1)S(1)}, bf16[1,1,32,8,256]{4,3,0,2,1:T(8,128)(2,1)S(1)}, u32[]{:S(2)}, u32[]{:S(2)}) collective-permute-start(bf16[1,1,32,8,256]{4,3,0,2,1:T(8,128)(2,1)S(1)} %get-tuple-element.5), channel_id=1, source_target_pairs={{0,7},{1,0},{2,1},{3,2},{4,3},{5,4},{6,5},{7,6},{8,15},{9,8},{10,9... | collective-permute-start | bytes 393224 | tf_op jit(solution)/shard_map/ppermute | solution.py:79
  64.9 3.2 %copy-start.3 = (bf16[256,256]{1,0:T(8,128)(2,1)S(1)}, bf16[256,256]{1,0:T(8,128)(2,1)}, u32[]{:S(2)}) copy-start(bf16[256,256]{1,0:T(8,128)(2,1)} %param.12) | copy-start | bytes 393220
  79.2 4.5 %copy-start.4 = (bf16[256,256]{1,0:T(8,128)(2,1)S(1)}, bf16[256,256]{1,0:T(8,128)(2,1)}, u32[]{:S(2)}) copy-start(bf16[256,256]{1,0:T(8,128)(2,1)} %param.14) | copy-start | bytes 393220
  120.5 0.9 copy-start.5
